TPU v7x, 512 devices: a whole 4x8x8 slice. The times are simulated.
512 devices in a mesh: seq: 32 (over y, x), head: 16 (over z, core).
Axes of the slice: x: 4, y: 8, z: 8, core: 2. Of those that a mesh axis runs over, the one named last changes fastest.
Arguments:
- queries: float32 [32, 8192, 128], P('head', 'seq'), may hold values from -8 to 8
- keys: float32 [32, 8192, 128], P('head', 'seq'), may hold values from -8 to 8
- values: float32 [32, 8192, 128], P('head', 'seq'), may hold values from -6 to 6
- output: float32 [32, 8192, 128], P('head', 'seq'), may hold values from -3 to 3
- grad_output: float32 [32, 8192, 128], P(None, ('seq', 'head')), may hold values from -6 to 6
- mid_offsets: int32 [32, 9], P('head'), may hold values from 0 to 3
- far_offsets: int32 [32], P('head'), may hold values from 0 to 31
- drop_local: int32 [32, 8192, 64], P('head', 'seq'), may hold values from 0 to 4095
- drop_mid: int32 [32, 2048, 64], P('head', 'seq'), may hold values from 0 to 4095
- drop_far: int32 [32, 256, 64], P('head'), may hold values from 0 to 4095
Outputs:
- grad_queries: float32 [32, 8192, 128], P(None, ('seq', 'head'))
- grad_keys: float32 [32, 8192, 128], P(None, ('seq', 'head'))
- grad_values: float32 [32, 8192, 128], P(None, ('seq', 'head'))
All inputs are finite; a program needn't handle non-finite values.
Results may differ from a plain program's by a relative error of at most 0.0003.
Values sent between devices are 32-bit elements; how exact they have to be, the bound alone decides.
No kernel may reach another device: no remote copies, remote signals or barrier semaphores. Data moves between devices by JAX's collectives and lax.ppermute only.
A program may use at most 64 MiB of HBM per device.

v0:
```python
import jax
import jax.numpy as jnp
from jax import lax
from jax.sharding import PartitionSpec as P

GROUP = 4
keep_level = 7
keep_scale = 8.0 / 7.0
highest = lax.Precision.HIGHEST


def shifted(value, axis, steps):
    count = lax.axis_size(axis)
    initial, last = (max(0, -steps), min(count, count - steps))
    return lax.ppermute(value, axis, [(source, source + steps) for source in range(initial, last)])


def unpack_keep(words):
    bit_starts = jnp.arange(4, dtype=jnp.int32) * 3
    levels = jnp.bitwise_and(jnp.right_shift(words[..., None], bit_starts), 7)
    kept = jnp.where(levels < keep_level, keep_scale, 0.0).astype(jnp.float32)
    return kept.reshape(words.shape[:-1] + (words.shape[-1] * 4,))


def masked_lse(scores, allowed):
    return jax.nn.logsumexp(jnp.where(allowed, scores, -jnp.inf), axis=-1)


def chosen_mask(offsets, stride, extra_dims):
    chosen = jnp.arange(stride, dtype=jnp.int32)[None, None, :] == offsets[:, None, None]
    return chosen.reshape(chosen.shape + (1,) * extra_dims)


def pick_rows(source, offsets, stride):
    split_rows = source.reshape(
        (source.shape[0], source.shape[1] // stride, stride) + source.shape[2:]
    )
    chosen = chosen_mask(offsets, stride, source.ndim - 2)
    return jnp.sum(jnp.where(chosen, split_rows, 0.0), axis=2)


def add_rows(target, addend, offsets, stride):
    split_rows = target.reshape(
        (target.shape[0], target.shape[1] // stride, stride) + target.shape[2:]
    )
    chosen = chosen_mask(offsets, stride, target.ndim - 2)
    return (split_rows + jnp.where(chosen, jnp.expand_dims(addend, 2), 0.0)).reshape(target.shape)


def merge_lse(target, addend, offsets, stride):
    split_rows = target.reshape((target.shape[0], target.shape[1] // stride, stride))
    chosen = chosen_mask(offsets, stride, 0)
    merged = jnp.where(chosen, jnp.logaddexp(split_rows, jnp.expand_dims(addend, 2)), split_rows)
    return merged.reshape(target.shape)


def score_terms(scores, allowed, lse_rows, delta_rows, kept, value_rows, grad_rows):
    probs = jnp.where(allowed, jnp.exp(scores - lse_rows[..., None]), 0.0)
    dropped = probs * kept
    grad_probs = jnp.einsum("hqd,hkd->hqk", grad_rows, value_rows, precision=highest) * kept
    return (dropped, probs * (grad_probs - delta_rows[..., None]))


def per_device(
    queries,
    keys,
    values,
    output,
    grad_output,
    mid_offsets,
    far_offsets,
    drop_local,
    drop_mid,
    drop_far,
):
    row_count = queries.shape[1]
    score_scale = queries.shape[2] ** (-0.5)
    cycle_size = lax.axis_size("seq")
    cycle_place = lax.axis_index("seq")
    grad_rows = lax.all_to_all(grad_output, "head", split_axis=0, concat_axis=1, tiled=True)
    delta = jnp.sum(grad_rows * output, axis=-1)
    row_order = jnp.arange(row_count, dtype=jnp.int32)
    local_scores = jnp.einsum("hqd,hkd->hqk", queries, keys, precision=highest) * score_scale
    local_allowed = (row_order[:, None] >= row_order[None, :])[None]
    total_lse = masked_lse(local_scores, local_allowed)
    quarter_rows = row_count // GROUP
    shifted_place = cycle_place + GROUP // 2
    group_pos = shifted_place % GROUP
    mid_off = lax.dynamic_index_in_dim(mid_offsets, shifted_place // GROUP, 1, keepdims=False)
    mid_q = pick_rows(queries, mid_off, GROUP)
    mid_k = pick_rows(keys, mid_off, GROUP)
    mid_v = pick_rows(values, mid_off, GROUP)
    mid_grad = pick_rows(grad_rows, mid_off, GROUP)
    mid_delta = pick_rows(delta, mid_off, GROUP)
    mid_pair = jnp.stack([mid_k, mid_v])
    quarter_order = jnp.arange(quarter_rows, dtype=jnp.int32)
    key_blocks = [mid_k]
    value_blocks = [mid_v]
    allowed_blocks = [quarter_order[:, None] >= quarter_order[None, :]]
    mid_words = unpack_keep(drop_mid)
    keep_blocks = [lax.dynamic_slice_in_dim(mid_words, group_pos * quarter_rows, quarter_rows, 2)]
    for distance in range(1, GROUP):
        received = shifted(mid_pair, "seq", distance)
        key_blocks.append(received[0])
        value_blocks.append(received[1])
        allowed_blocks.append(
            jnp.broadcast_to(
                (group_pos >= distance) & (cycle_place >= distance), (quarter_rows, quarter_rows)
            )
        )
        keep_blocks.append(
            lax.dynamic_slice_in_dim(
                mid_words, jnp.maximum(group_pos - distance, 0) * quarter_rows, quarter_rows, 2
            )
        )
    mid_keys_all = jnp.concatenate(key_blocks, axis=1)
    mid_values_all = jnp.concatenate(value_blocks, axis=1)
    mid_allowed = jnp.concatenate(allowed_blocks, axis=1)[None]
    mid_keep = jnp.concatenate(keep_blocks, axis=2)
    mid_scores = jnp.einsum("hqd,hkd->hqk", mid_q, mid_keys_all, precision=highest) * score_scale
    mid_lse = masked_lse(mid_scores, mid_allowed)
    far_rows = row_count // cycle_size
    far_q = pick_rows(queries, far_offsets, cycle_size)
    far_k = pick_rows(keys, far_offsets, cycle_size)
    far_v = pick_rows(values, far_offsets, cycle_size)
    far_grad = pick_rows(grad_rows, far_offsets, cycle_size)
    far_delta = pick_rows(delta, far_offsets, cycle_size)
    far_all = lax.all_gather(jnp.stack([far_k, far_v]), "seq", axis=2, tiled=True)
    own_index = cycle_place * far_rows + jnp.arange(far_rows, dtype=jnp.int32)
    far_allowed = (row_order[None, :] <= own_index[:, None])[None]
    far_keep = unpack_keep(lax.dynamic_slice_in_dim(drop_far, cycle_place * far_rows, far_rows, 1))
    far_scores = jnp.einsum("hqd,hkd->hqk", far_q, far_all[0], precision=highest) * score_scale
    far_lse = masked_lse(far_scores, far_allowed)
    total_lse = merge_lse(total_lse, mid_lse, mid_off, GROUP)
    total_lse = merge_lse(total_lse, far_lse, far_offsets, cycle_size)
    local_keep = unpack_keep(drop_local)
    dropped, grad_scores = score_terms(
        local_scores, local_allowed, total_lse, delta, local_keep, values, grad_rows
    )
    grad_v = jnp.einsum("hqk,hqd->hkd", dropped, grad_rows, precision=highest)
    grad_q = jnp.einsum("hqk,hkd->hqd", grad_scores, keys, precision=highest) * score_scale
    grad_k = jnp.einsum("hqk,hqd->hkd", grad_scores, queries, precision=highest) * score_scale
    mid_lse_rows = pick_rows(total_lse, mid_off, GROUP)
    dropped, grad_scores = score_terms(
        mid_scores, mid_allowed, mid_lse_rows, mid_delta, mid_keep, mid_values_all, mid_grad
    )
    mid_gv = jnp.einsum("hqk,hqd->hkd", dropped, mid_grad, precision=highest)
    mid_gq = jnp.einsum("hqk,hkd->hqd", grad_scores, mid_keys_all, precision=highest) * score_scale
    mid_gk = jnp.einsum("hqk,hqd->hkd", grad_scores, mid_q, precision=highest) * score_scale
    own_gk = mid_gk[:, :quarter_rows]
    own_gv = mid_gv[:, :quarter_rows]
    for distance in range(1, GROUP):
        outgoing = jnp.stack(
            [
                mid_gk[:, distance * quarter_rows : (distance + 1) * quarter_rows],
                mid_gv[:, distance * quarter_rows : (distance + 1) * quarter_rows],
            ]
        )
        returned = shifted(outgoing, "seq", -distance)
        own_gk = own_gk + returned[0]
        own_gv = own_gv + returned[1]
    far_lse_rows = pick_rows(total_lse, far_offsets, cycle_size)
    dropped, grad_scores = score_terms(
        far_scores, far_allowed, far_lse_rows, far_delta, far_keep, far_all[1], far_grad
    )
    far_gq = jnp.einsum("hqk,hkd->hqd", grad_scores, far_all[0], precision=highest) * score_scale
    far_gv_all = jnp.einsum("hqk,hqd->hkd", dropped, far_grad, precision=highest)
    far_gk_all = jnp.einsum("hqk,hqd->hkd", grad_scores, far_q, precision=highest) * score_scale
    shares = lax.psum_scatter(
        jnp.stack([far_gk_all, far_gv_all]), "seq", scatter_dimension=2, tiled=True
    )
    far_gk = shares[0]
    far_gv = shares[1]
    grad_q = add_rows(add_rows(grad_q, mid_gq, mid_off, GROUP), far_gq, far_offsets, cycle_size)
    grad_k = add_rows(add_rows(grad_k, own_gk, mid_off, GROUP), far_gk, far_offsets, cycle_size)
    grad_v = add_rows(add_rows(grad_v, own_gv, mid_off, GROUP), far_gv, far_offsets, cycle_size)
    result = lax.all_to_all(
        jnp.stack([grad_q, grad_k, grad_v]), "head", split_axis=2, concat_axis=1, tiled=True
    )
    return (result[0], result[1], result[2])


def solution(mesh):
    placed = (
        P("head", "seq", None),
        P("head", "seq", None),
        P("head", "seq", None),
        P("head", "seq", None),
        P(None, ("seq", "head"), None),
        P("head", None),
        P("head"),
        P("head", "seq", None),
        P("head", "seq", None),
        P("head", None, None),
    )
    return jax.shard_map(
        per_device,
        mesh=mesh,
        in_specs=placed,
        out_specs=(
            P(None, ("seq", "head"), None),
            P(None, ("seq", "head"), None),
            P(None, ("seq", "head"), None),
        ),
        check_vma=False,
    )
```

profile of v0, /device:TPU:1, one launch (start us, length us, event | category | flops | bytes accessed | tf_op | source)
XLA Modules:
  0.0 363.3 jit_solution(801214255351252391)
XLA Ops:
  7.2 12.0 %all-to-all-start = ((f32[32,16,128]{2,1,0:T(8,128)}), f32[32,16,128]{2,1,0:T(8,128)S(1)}, u32[]{:S(2)}, u32[]{:S(2)}) async-start(f32[32,16,128]{2,1,0:T(8,128)} %param.14), calls=%async_computation | async-start | bytes 524288 | tf_op jit(solution)/shard_map/all_to_all | solution.py:80
  21.9 33.7 %all_gather.3 = f32[2,2,256,128]{3,2,1,0:T(8,128)S(1)} all-gather(f32[2,2,8,128]{3,2,1,0:T(8,128)S(1)} %pad_maximum_fusion.10), channel_id=1, replica_groups=mesh['seq'=32,'head'=16] {'seq'}, dimensions={2}, use_global_device_ids=true | all-gather | bytes 540672 | tf_op jit(solution)/shard_map/all_gather | solution.py:128
  56.9 0.7 exponential_reduce_fusion
  58.3 0.8 constant_dynamic-slice_fusion.4
  60.5 0.7 broadcast_in_dim.374
  61.2 0.7 reduce_max.32
  61.9 0.7 broadcast_in_dim.356
  62.7 0.7 copy.55
  65.9 0.9 copy-done.6
  67.7 0.8 select_reduce_fusion.1
  68.5 4.0 %collective-permute-start.2 = (f32[2,2,64,128]{3,2,1,0:T(8,128)S(1)}, f32[2,2,64,128]{3,2,1,0:T(8,128)}, u32[]{:S(2)}, u32[]{:S(2)}) collective-permute-start(f32[2,2,64,128]{3,2,1,0:T(8,128)S(1)} %pad_maximum_fusion.5), channel_id=1, source_target_pairs={{0,48},{16,64},{32,80},{48,96},{64,112},{80,128},{96,144},{112,160... | collective-permute-start | bytes 393224 | tf_op jit(solution)/shard_map/ppermute | solution.py:15
  72.5 2.5 collective-permute-start.1
  75.0 1.8 collective-permute-start
  78.3 1.5 slice_bitcast_fusion.17
  84.1 0.8 select_reduce_fusion.11
  87.2 0.7 fusion.27
  90.3 0.8 pad_maximum_fusion.1
  91.2 1.3 collective-permute-start.4
  92.5 1.3 collective-permute-start.5
  93.8 1.6 collective-permute-start.3
  96.4 0.7 fusion.1
  97.5 1.3 collective-permute-done.4
  98.8 2.1 collective-permute-done.5
  101.1 212.0 %reduce-scatter.2.cloned.1.call-done = f32[2,2,8,128]{3,2,1,0:T(8,128)} async-done(((f32[2,2,256,128]{3,2,1,0:T(8,128)}), f32[2,2,8,128]{3,2,1,0:T(8,128)}) %reduce-scatter.2.cloned.1.call-update) | async-done | bytes 16400 | tf_op jit(solution)/shard_map/reduce_scatter | solution.py:169
  313.1 0.7 slice_bitcast_fusion.24
  313.8 0.7 copy-done.36
  314.7 0.8 fusion.10
  315.5 1.0 fusion.5
  317.9 36.0 %all_to_all.33 = f32[3,2,256,128]{3,1,0,2:T(2,128)S(1)} all-to-all(f32[3,2,256,128]{3,1,0,2:T(2,128)S(1)} %copy.56), channel_id=1, replica_groups=mesh['seq'=32,'head'=16] {'head'}, dimensions={2} | all-to-all | bytes 1572864 | tf_op jit(solution)/shard_map/all_to_all | solution.py:177
  354.3 0.7 copy.59
  355.0 0.7 copy.58
  355.7 0.7 copy.57
  (190 shorter events, 23.1 us)
Async XLA Ops:
  7.2 51.9 %copy-start = (s32[2,256,64]{1,2,0:T(8,128)S(1)}, s32[2,256,64]{1,2,0:T(8,128)}, u32[]{:S(2)}) copy-start(s32[2,256,64]{1,2,0:T(8,128)} %param.19) | copy-start | bytes 393220
  7.2 58.7 %all-to-all-start = ((f32[32,16,128]{2,1,0:T(8,128)}), f32[32,16,128]{2,1,0:T(8,128)S(1)}, u32[]{:S(2)}, u32[]{:S(2)}) async-start(f32[32,16,128]{2,1,0:T(8,128)} %param.14), calls=%async_computation | async-start | bytes 524288 | tf_op jit(solution)/shard_map/all_to_all | solution.py:80
  19.2 294.0 %reduce-scatter.2.cloned.1.call-start = ((), (), s32[]{:S(2)}) async-start(), calls=%async_computation.3 | async-start | bytes 540672 | tf_op jit(solution)/shard_map/reduce_scatter | solution.py:169
  19.3 0.9 copy-start.50
  19.3 37.6 %copy-start.4 = (pred[256,256]{0,1:T(8,128)(4,1)}, pred[256,256]{0,1:T(8,128)(4,1)S(1)}, u32[]{:S(2)}) copy-start(pred[256,256]{0,1:T(8,128)(4,1)S(1)} %iota_compare_fusion) | copy-start | bytes 196612
  19.3 1.1 copy-start.17
  20.2 41.7 %copy-start.39 = (pred[2,4]{1,0:T(4,128)(4,1)}, pred[2,4]{1,0:T(4,128)(4,1)S(1)}, u32[]{:S(2)}) copy-start(pred[2,4]{1,0:T(4,128)(4,1)S(1)} %iota_compare_fusion.3) | copy-start | bytes 28
  20.3 38.9 %copy-start.42 = (pred[2,32]{1,0:T(4,128)(4,1)}, pred[2,32]{1,0:T(4,128)(4,1)S(1)}, u32[]{:S(2)}) copy-start(pred[2,32]{1,0:T(4,128)(4,1)S(1)} %iota_compare_fusion.4) | copy-start | bytes 196
  20.4 35.7 %copy-start.26 = (pred[8,256]{1,0:T(8,128)(4,1)}, pred[8,256]{1,0:T(8,128)(4,1)S(1)}, u32[]{:S(2)}) copy-start(pred[8,256]{1,0:T(8,128)(4,1)S(1)} %iota_compare_fusion.2) | copy-start | bytes 6148
  20.5 36.4 %copy-start.33 = (s32[256]{0:T(256)}, s32[256]{0:T(256)S(1)}, u32[]{:S(2)}) copy-start(s32[256]{0:T(256)S(1)} %shift_right_arithmetic.63) | copy-start | bytes 3076
  20.5 1.0 copy-start.3
  20.6 1.0 copy-start.2
  20.7 1.0 copy-start.1
  21.9 33.8 %copy-start.14 = (f32[2,8,128]{2,1,0:T(8,128)}, f32[2,8,128]{2,1,0:T(8,128)S(1)}, u32[]{:S(2)}) copy-start(f32[2,8,128]{2,1,0:T(8,128)S(1)} %get-tuple-element.12) | copy-start | bytes 24580
  56.9 4.4 %copy-start.28 = (f32[2,256]{1,0:T(2,128)}, f32[2,256]{1,0:T(2,128)S(1)}, u32[]{:S(2)}) copy-start(f32[2,256]{1,0:T(2,128)S(1)} %get-tuple-element.45) | copy-start | bytes 6148
  62.7 2.2 copy-start.13
  65.9 1.0 copy-start.6
  68.5 8.3 %copy-start.32 = (pred[2,16,16]{2,1,0:T(8,128)(4,1)S(1)}, pred[2,16,16]{2,1,0:T(8,128)(4,1)}, u32[]{:S(2)}) copy-start(pred[2,16,16]{2,1,0:T(8,128)(4,1)} %broadcast_in_dim.383) | copy-start | bytes 1540
  68.5 9.8 %collective-permute-start.2 = (f32[2,2,64,128]{3,2,1,0:T(8,128)S(1)}, f32[2,2,64,128]{3,2,1,0:T(8,128)}, u32[]{:S(2)}, u32[]{:S(2)}) collective-permute-start(f32[2,2,64,128]{3,2,1,0:T(8,128)S(1)} %pad_maximum_fusion.5), channel_id=1, source_target_pairs={{0,48},{16,64},{32,80},{48,96},{64,112},{80,128},{96,144},{112,160... | collective-permute-start | bytes 393224 | tf_op jit(solution)/shard_map/ppermute | solution.py:15
  72.5 7.3 %collective-permute-start.1 = (f32[2,2,64,128]{3,2,1,0:T(8,128)S(1)}, f32[2,2,64,128]{3,2,1,0:T(8,128)S(1)}, u32[]{:S(2)}, u32[]{:S(2)}) collective-permute-start(f32[2,2,64,128]{3,2,1,0:T(8,128)S(1)} %pad_maximum_fusion.5), channel_id=1, source_target_pairs={{0,32},{16,48},{32,64},{48,80},{64,96},{80,112},{96,128},{112,144}... | collective-permute-start | bytes 393224 | tf_op jit(solution)/shard_map/ppermute | solution.py:15
  75.0 5.5 %collective-permute-start = (f32[2,2,64,128]{3,2,1,0:T(8,128)S(1)}, f32[2,2,64,128]{3,2,1,0:T(8,128)S(1)}, u32[]{:S(2)}, u32[]{:S(2)}) collective-permute-start(f32[2,2,64,128]{3,2,1,0:T(8,128)S(1)} %pad_maximum_fusion.5), channel_id=1, source_target_pairs={{0,16},{16,32},{32,48},{48,64},{64,80},{80,96},{96,112},{112,128},... | collective-permute-start | bytes 393224 | tf_op jit(solution)/shard_map/ppermute | solution.py:15
  82.0 1.4 copy-start.7
  84.8 1.8 copy-start.44
  86.3 0.9 copy-start.10
  86.3 0.9 copy-start.11
  87.2 0.9 copy-start.23
  87.2 0.9 copy-start.24
  87.2 0.9 copy-start.48
  91.2 7.6 %collective-permute-start.4 = (f32[2,2,64,128]{3,2,1,0:T(8,128)S(1)}, f32[2,2,64,128]{3,2,1,0:T(8,128)S(1)}, u32[]{:S(2)}, u32[]{:S(2)}) collective-permute-start(f32[2,2,64,128]{3,2,1,0:T(8,128)S(1)} %pad_maximum_fusion.8), channel_id=1, source_target_pairs={{32,0},{48,16},{64,32},{80,48},{96,64},{112,80},{128,96},{144,112}... | collective-permute-start | bytes 393224 | tf_op jit(solution)/shard_map/ppermute | solution.py:15
  92.5 8.4 %collective-permute-start.5 = (f32[2,2,64,128]{3,2,1,0:T(8,128)S(1)}, f32[2,2,64,128]{3,2,1,0:T(8,128)S(1)}, u32[]{:S(2)}, u32[]{:S(2)}) collective-permute-start(f32[2,2,64,128]{3,2,1,0:T(8,128)S(1)} %pad_maximum_fusion.9), channel_id=1, source_target_pairs={{48,0},{64,16},{80,32},{96,48},{112,64},{128,80},{144,96},{160,112... | collective-permute-start | bytes 393224 | tf_op jit(solution)/shard_map/ppermute | solution.py:15
  93.8 1.9 copy-start.5
  93.8 7.2 %collective-permute-start.3 = (f32[2,2,64,128]{3,2,1,0:T(8,128)S(1)}, f32[2,2,64,128]{3,2,1,0:T(8,128)S(1)}, u32[]{:S(2)}, u32[]{:S(2)}) collective-permute-start(f32[2,2,64,128]{3,2,1,0:T(8,128)S(1)} %pad_maximum_fusion.7), channel_id=1, source_target_pairs={{16,0},{32,16},{48,32},{64,48},{80,64},{96,80},{112,96},{128,112},... | collective-permute-start | bytes 393224 | tf_op jit(solution)/shard_map/ppermute | solution.py:15
  (27 other events, 19.2 us)
Sparse Core Ops, SparseCore 0:
  91.3 221.8 reduce-scatter.1
where the time goes:
time: 364 us; the launch traced here: 363 us
  waiting for transfers between devices  216 us (59%)
  blocking collectives  69.7 us (19%)
  starting transfers between devices  24.5 us (7%)
  local copies, waits for them, and re-layouts  23.7 us (7%)
  between operations  14.9 us (4%)
  matrix products  8.36 us (2%)
  other arithmetic  6.66 us (2%)
    reduce_scatter x1, waiting for transfers between devices, per_device(): lax.psum_scatter(jnp.stack([far_gk_all, far_gv_all]), 'seq', scatter_dime...  212 us
    all_to_all x1, blocking collectives, per_device(): lax.all_to_all(jnp.stack([grad_q, grad_k, grad_v]), 'head', split_axis=2,...  36 us
    all_gather x1, blocking collectives, per_device(): lax.all_gather(jnp.stack([far_k, far_v]), 'seq', axis=2, tiled=True)  33.7 us
    ppermute x6, starting transfers between devices, shifted(): lax.ppermute(value, axis, [(source, source + steps) for source in range(i...  12.5 us
    all_to_all x1, starting transfers between devices, per_device(): lax.all_to_all(grad_output, 'head', split_axis=0, concat_axis=1, tiled=True)  12 us
    unnamed x103, local copies, waits for them, and re-layouts  8.8 us
  transfers between devices with their start and end apart: 8, of which 4 were waited for; matrix products, arithmetic and copies ran while one was open for 4% of the time, Pallas kernels for 0%

commit v1 on v0

--- a/solution.py
+++ b/solution.py
@@ -125,7 +125,9 @@
     far_v = pick_rows(values, far_offsets, cycle_size)
     far_grad = pick_rows(grad_rows, far_offsets, cycle_size)
     far_delta = pick_rows(delta, far_offsets, cycle_size)
-    far_all = lax.all_gather(jnp.stack([far_k, far_v]), "seq", axis=2, tiled=True)
+    part = jnp.stack([far_k, far_v])
+    stack = jnp.stack([part] * lax.axis_size("seq"))
+    far_all = jnp.concatenate(lax.all_to_all(stack, "seq", 0, 0), axis=2)
     own_index = cycle_place * far_rows + jnp.arange(far_rows, dtype=jnp.int32)
     far_allowed = (row_order[None, :] <= own_index[:, None])[None]
     far_keep = unpack_keep(lax.dynamic_slice_in_dim(drop_far, cycle_place * far_rows, far_rows, 1))

time: 364 us -> 339 us (0.931)
  blocking collectives: 69.7 us -> 36.2 us
  starting transfers between devices: 24.5 us -> 36 us
    all_gather x1 -> x0, blocking collectives: 33.7 us -> none  [per_device(): lax.all_gather(jnp.stack([far_k, far_v]), 'seq', axis=2, tiled=True)]
    all_to_all x0 -> x1, starting transfers between devices: none -> 9.67 us  [per_device(): far_all = jnp.concatenate(lax.all_to_all(stack, 'seq', 0, 0), axis=2)]
    reduce_scatter x1, waiting for transfers between devices: 212 us -> 203 us  [per_device(): lax.psum_scatter(jnp.stack([far_gk_all, far_gv_all]), 'seq', scatter_dime...]
    unnamed x103 -> x81, local copies, waits for them, and re-layouts: 8.8 us -> 10.1 us
  transfers between devices with their start and end apart: 8 -> 9, of which waited for: 4 -> 5; matrix products, arithmetic and copies ran while one was open for 4% -> 4% of each run, Pallas kernels for 0% -> 0%
where the time goes in v1:
time: 339 us; the launch traced here: 338 us
  waiting for transfers between devices  213 us (63%)
  blocking collectives  36.2 us (11%)
  starting transfers between devices  36 us (11%)
  local copies, waits for them, and re-layouts  23.6 us (7%)
  between operations  14.7 us (4%)
  matrix products  8.37 us (2%)
  other arithmetic  6.06 us (2%)
    reduce_scatter x1, waiting for transfers between devices, per_device(): lax.psum_scatter(jnp.stack([far_gk_all, far_gv_all]), 'seq', scatter_dime...  203 us
    all_to_all x1, blocking collectives, per_device(): lax.all_to_all(jnp.stack([grad_q, grad_k, grad_v]), 'head', split_axis=2,...  36.2 us
    ppermute x6, starting transfers between devices, shifted(): lax.ppermute(value, axis, [(source, source + steps) for source in range(i...  14.3 us
    all_to_all x1, starting transfers between devices, per_device(): lax.all_to_all(grad_output, 'head', split_axis=0, concat_axis=1, tiled=True)  12 us
    unnamed x81, local copies, waits for them, and re-layouts  10.1 us
    all_to_all x1, starting transfers between devices, per_device(): far_all = jnp.concatenate(lax.all_to_all(stack, 'seq', 0, 0), axis=2)  9.67 us
  transfers between devices with their start and end apart: 9, of which 5 were waited for; matrix products, arithmetic and copies ran while one was open for 4% of the time, Pallas kernels for 0%

profile of v1, /device:TPU:1, one launch (start us, length us, event | category | flops | bytes accessed | tf_op | source)
XLA Modules:
  0.0 337.8 jit_solution(2791056139395050232)
XLA Ops:
  7.2 12.0 %all-to-all-start.1 = ((f32[32,16,128]{2,1,0:T(8,128)}), f32[32,16,128]{2,1,0:T(8,128)S(1)}, u32[]{:S(2)}, u32[]{:S(2)}) async-start(f32[32,16,128]{2,1,0:T(8,128)} %param.14), calls=%async_computation.1 | async-start | bytes 524288 | tf_op jit(solution)/shard_map/all_to_all | solution.py:80
  20.7 0.8 copy-done.2
  22.8 0.7 exponential_reduce_fusion
  23.5 0.8 constant_dynamic-slice_fusion.4
  25.4 0.7 broadcast_in_dim.356
  26.2 0.8 copy-done.9
  27.5 3.3 all-to-all-done.1
  30.9 0.8 stack.46
  31.7 9.7 %all-to-all-start = ((f32[32,2,2,8,128]{4,3,2,1,0:T(8,128)}), f32[32,2,2,8,128]{4,3,2,1,0:T(8,128)S(1)}, u32[]{:S(2)}, u32[]{:S(2)}) async-start(f32[32,2,2,8,128]{4,3,2,1,0:T(8,128)} %stack.46), calls=%async_computation | async-start | bytes 1048576 | tf_op jit(solution)/shard_map/all_to_all | solution.py:130
  41.5 0.9 copy-done.4
  43.3 0.8 select_reduce_fusion.1
  44.1 5.0 %collective-permute-start.2 = (f32[2,2,64,128]{3,2,1,0:T(8,128)S(1)}, f32[2,2,64,128]{3,2,1,0:T(8,128)}, u32[]{:S(2)}, u32[]{:S(2)}) collective-permute-start(f32[2,2,64,128]{3,2,1,0:T(8,128)S(1)} %pad_maximum_fusion.5), channel_id=1, source_target_pairs={{0,48},{16,64},{32,80},{48,96},{64,112},{80,128},{96,144},{112,160... | collective-permute-start | bytes 393224 | tf_op jit(solution)/shard_map/ppermute | solution.py:15
  49.1 3.4 collective-permute-start.1
  52.5 1.9 collective-permute-start
  55.9 1.5 slice_bitcast_fusion.12
  58.1 0.9 collective-permute-done
  64.6 0.8 select_reduce_fusion.11
  70.9 0.8 pad_maximum_fusion.1
  71.8 1.3 collective-permute-start.4
  73.1 1.3 collective-permute-start.5
  74.4 1.5 collective-permute-start.3
  76.8 0.7 fusion.1
  78.1 3.2 collective-permute-done.4
  81.2 2.7 collective-permute-done.5
  84.0 202.7 %reduce-scatter.2.cloned.1.call-done = f32[2,2,8,128]{3,2,1,0:T(8,128)} async-done(((f32[2,2,256,128]{3,2,1,0:T(8,128)}), f32[2,2,8,128]{3,2,1,0:T(8,128)}) %reduce-scatter.2.cloned.1.call-update) | async-done | bytes 16400 | tf_op jit(solution)/shard_map/reduce_scatter | solution.py:171
  286.7 0.7 slice_bitcast_fusion.19
  288.9 0.8 fusion.10
  289.8 1.0 fusion.5
  292.1 36.2 %all_to_all.38 = f32[3,2,256,128]{3,1,0,2:T(2,128)S(1)} all-to-all(f32[3,2,256,128]{3,1,0,2:T(2,128)S(1)} %copy.62), channel_id=1, replica_groups=mesh['seq'=32,'head'=16] {'head'}, dimensions={2} | all-to-all | bytes 1572864 | tf_op jit(solution)/shard_map/all_to_all | solution.py:179
  328.8 0.7 copy.65
  329.5 0.7 copy.64
  330.2 0.7 copy.63
  (171 shorter events, 23.3 us)
Async XLA Ops:
  7.2 15.5 %copy-start = (s32[2,256,64]{1,2,0:T(8,128)S(1)}, s32[2,256,64]{1,2,0:T(8,128)}, u32[]{:S(2)}) copy-start(s32[2,256,64]{1,2,0:T(8,128)} %param.19) | copy-start | bytes 393220
  7.2 23.7 %all-to-all-start.1 = ((f32[32,16,128]{2,1,0:T(8,128)}), f32[32,16,128]{2,1,0:T(8,128)S(1)}, u32[]{:S(2)}, u32[]{:S(2)}) async-start(f32[32,16,128]{2,1,0:T(8,128)} %param.14), calls=%async_computation.1 | async-start | bytes 524288 | tf_op jit(solution)/shard_map/all_to_all | solution.py:80
  19.2 0.9 copy-start.39
  19.2 1.2 copy-start.12
  20.1 23.2 %copy-start.32 = (pred[2,4]{1,0:T(4,128)(4,1)}, pred[2,4]{1,0:T(4,128)(4,1)S(1)}, u32[]{:S(2)}) copy-start(pred[2,4]{1,0:T(4,128)(4,1)S(1)} %iota_compare_fusion.3) | copy-start | bytes 28
  20.2 4.2 %copy-start.34 = (pred[2,32]{1,0:T(4,128)(4,1)}, pred[2,32]{1,0:T(4,128)(4,1)S(1)}, u32[]{:S(2)}) copy-start(pred[2,32]{1,0:T(4,128)(4,1)S(1)} %iota_compare_fusion.4) | copy-start | bytes 196
  20.5 1.0 copy-start.2
  20.6 1.0 copy-start.1
  21.5 0.9 copy-start.3
  26.1 0.9 copy-start.9
  31.7 30.0 %all-to-all-start = ((f32[32,2,2,8,128]{4,3,2,1,0:T(8,128)}), f32[32,2,2,8,128]{4,3,2,1,0:T(8,128)S(1)}, u32[]{:S(2)}, u32[]{:S(2)}) async-start(f32[32,2,2,8,128]{4,3,2,1,0:T(8,128)} %stack.46), calls=%async_computation | async-start | bytes 1048576 | tf_op jit(solution)/shard_map/all_to_all | solution.py:130
  41.4 245.3 %reduce-scatter.2.cloned.1.call-start = ((), (), s32[]{:S(2)}) async-start(), calls=%async_computation.4 | async-start | bytes 540672 | tf_op jit(solution)/shard_map/reduce_scatter | solution.py:171
  41.4 1.0 copy-start.4
  44.1 11.8 %collective-permute-start.2 = (f32[2,2,64,128]{3,2,1,0:T(8,128)S(1)}, f32[2,2,64,128]{3,2,1,0:T(8,128)}, u32[]{:S(2)}, u32[]{:S(2)}) collective-permute-start(f32[2,2,64,128]{3,2,1,0:T(8,128)S(1)} %pad_maximum_fusion.5), channel_id=1, source_target_pairs={{0,48},{16,64},{32,80},{48,96},{64,112},{80,128},{96,144},{112,160... | collective-permute-start | bytes 393224 | tf_op jit(solution)/shard_map/ppermute | solution.py:15
  49.1 8.3 %collective-permute-start.1 = (f32[2,2,64,128]{3,2,1,0:T(8,128)S(1)}, f32[2,2,64,128]{3,2,1,0:T(8,128)S(1)}, u32[]{:S(2)}, u32[]{:S(2)}) collective-permute-start(f32[2,2,64,128]{3,2,1,0:T(8,128)S(1)} %pad_maximum_fusion.5), channel_id=1, source_target_pairs={{0,32},{16,48},{32,64},{48,80},{64,96},{80,112},{96,128},{112,144}... | collective-permute-start | bytes 393224 | tf_op jit(solution)/shard_map/ppermute | solution.py:15
  52.5 6.5 %collective-permute-start = (f32[2,2,64,128]{3,2,1,0:T(8,128)S(1)}, f32[2,2,64,128]{3,2,1,0:T(8,128)S(1)}, u32[]{:S(2)}, u32[]{:S(2)}) collective-permute-start(f32[2,2,64,128]{3,2,1,0:T(8,128)S(1)} %pad_maximum_fusion.5), channel_id=1, source_target_pairs={{0,16},{16,32},{32,48},{48,64},{64,80},{80,96},{96,112},{112,128},... | collective-permute-start | bytes 393224 | tf_op jit(solution)/shard_map/ppermute | solution.py:15
  57.4 2.2 copy-start.13
  58.1 1.6 copy-start.15
  63.9 1.6 copy-start.8
  64.6 0.9 copy-start.5
  64.6 0.9 copy-start.6
  64.6 0.9 copy-start.7
  65.5 0.8 copy-start.19
  65.6 0.9 copy-start.20
  65.6 0.9 copy-start.21
  71.8 9.4 %collective-permute-start.4 = (f32[2,2,64,128]{3,2,1,0:T(8,128)S(1)}, f32[2,2,64,128]{3,2,1,0:T(8,128)S(1)}, u32[]{:S(2)}, u32[]{:S(2)}) collective-permute-start(f32[2,2,64,128]{3,2,1,0:T(8,128)S(1)} %pad_maximum_fusion.8), channel_id=1, source_target_pairs={{32,0},{48,16},{64,32},{80,48},{96,64},{112,80},{128,96},{144,112}... | collective-permute-start | bytes 393224 | tf_op jit(solution)/shard_map/ppermute | solution.py:15
  73.1 10.8 %collective-permute-start.5 = (f32[2,2,64,128]{3,2,1,0:T(8,128)S(1)}, f32[2,2,64,128]{3,2,1,0:T(8,128)S(1)}, u32[]{:S(2)}, u32[]{:S(2)}) collective-permute-start(f32[2,2,64,128]{3,2,1,0:T(8,128)S(1)} %pad_maximum_fusion.9), channel_id=1, source_target_pairs={{48,0},{64,16},{80,32},{96,48},{112,64},{128,80},{144,96},{160,112... | collective-permute-start | bytes 393224 | tf_op jit(solution)/shard_map/ppermute | solution.py:15
  74.4 9.5 %collective-permute-start.3 = (f32[2,2,64,128]{3,2,1,0:T(8,128)S(1)}, f32[2,2,64,128]{3,2,1,0:T(8,128)S(1)}, u32[]{:S(2)}, u32[]{:S(2)}) collective-permute-start(f32[2,2,64,128]{3,2,1,0:T(8,128)S(1)} %pad_maximum_fusion.7), channel_id=1, source_target_pairs={{16,0},{32,16},{48,32},{64,48},{80,64},{96,80},{112,96},{128,112},... | collective-permute-start | bytes 393224 | tf_op jit(solution)/shard_map/ppermute | solution.py:15
  76.8 0.9 copy-start.11
  76.8 0.9 copy-start.14
  76.8 0.9 copy-start.16
  76.8 1.0 copy-start.18
  (17 other events, 11.5 us)
Sparse Core Ops, SparseCore 0:
  71.9 214.7 reduce-scatter.1
